TPU v7x, 256 devices: a whole 4x4x8 slice. The times are simulated.
256 devices in a mesh: blk: 16 (over y_lo, z), tgt: 4 (over y_hi, core), sec: 4 (over x).
Axes of the slice: x: 4, y: 4 (y_hi: 2, y_lo: 2; y = y_hi * 2 + y_lo), z: 8, core: 2. Of those that a mesh axis runs over, the one named last changes fastest.
Arguments:
- modal_loads: bfloat16 [4096, 128], P('blk'), may hold values from -6 to 6
- receptance: bfloat16 [2, 4096, 4096], P(None, ('tgt', 'sec'), 'blk'), may hold values from -0.0625 to 0.0625
- shapes: bfloat16 [32768, 8, 128], P(('blk', 'tgt', 'sec')), may hold values from -0.1875 to 0.1875
- coupling: int32 [256, 8], P(('blk', 'tgt', 'sec')), may hold values from 0 to 31, all different within a row
- panel_coords: float32 [3, 32768], P(None, ('blk', 'tgt', 'sec')), may hold values from 0 to 1
- panel_areas: float32 [32768], P(('blk', 'tgt', 'sec')), may hold values from 0.1 to 1
Outputs:
- new_loads: float32 [4096, 128], P(('blk', 'tgt', 'sec'))
- pressure: bfloat16 [32768, 128], P(('blk', 'tgt', 'sec'))
Inputs may be any that keep to these rules, and one draw needn't show every extreme that they name: `coupling`: each row names 8 different mode blocks; every mode block is named by some row.
All inputs are finite; a program needn't handle non-finite values.
Results may differ from a plain program's by a relative error of at most 0.009.
Values may be sent and summed in bfloat16 or wider, within the bound.
A program may use at most 64 MiB of HBM per device.

v0:
```python
import math

import jax
import jax.numpy as jnp
from jax import lax
from jax.sharding import PartitionSpec as P

wave_number = 40.0


def rotate_combine(leading, second):
    half_width = leading.shape[1] // 2
    return jnp.concatenate(
        [
            leading[:, :half_width] - second[:, half_width:],
            leading[:, half_width:] + second[:, :half_width],
        ],
        axis=1,
    )


def pressure_block(target_geometry, source_geometry, source_vel, total_panels):
    delta_x = target_geometry[0][:, None] - source_geometry[0][None, :]
    delta_y = target_geometry[1][:, None] - source_geometry[1][None, :]
    delta_z = target_geometry[2][:, None] - source_geometry[2][None, :]
    source_area = source_geometry[3][None, :]
    distance = jnp.sqrt(
        delta_x * delta_x + delta_y * delta_y + delta_z * delta_z + source_area / total_panels
    )
    weight = source_area / (distance * math.sqrt(total_panels))
    phase_angle = wave_number * distance
    kernel = jnp.concatenate(
        [
            (jnp.cos(phase_angle) * weight).astype(jnp.bfloat16),
            (jnp.sin(phase_angle) * weight).astype(jnp.bfloat16),
        ],
        axis=0,
    )
    products = lax.dot_general(
        kernel, source_vel, (((1,), (1,)), ((), ())), preferred_element_type=jnp.float32
    )
    target_count = target_geometry.shape[1]
    return rotate_combine(products[:target_count], products[target_count:])


def on_device(modal_loads, receptance, shapes, coupling, panel_coords, panel_areas):
    pan_dev = panel_coords.shape[1]
    case_width = modal_loads.shape[1]
    device_count = lax.axis_size("blk") * lax.axis_size("tgt") * lax.axis_size("sec")
    total_panels = float(pan_dev * device_count)
    row_share = receptance.shape[1]
    stacked = jnp.dot(
        receptance.reshape(2 * row_share, receptance.shape[2]),
        modal_loads,
        preferred_element_type=jnp.float32,
    )
    modal_sum = rotate_combine(stacked[:row_share], stacked[row_share:])
    modal_sum = lax.psum(modal_sum, "blk")
    amplitudes = lax.all_gather(modal_sum.astype(jnp.bfloat16), ("tgt", "sec"), axis=0, tiled=True)
    mode_block = shapes.shape[2]
    blocks = amplitudes.reshape(-1, mode_block, case_width)
    chosen = blocks[coupling]
    block_count = coupling.shape[0]
    shaped = shapes.reshape(block_count, -1, shapes.shape[1], mode_block)
    vel_t = (
        jnp.einsum("bpkm,bkmc->cbp", shaped, chosen, preferred_element_type=jnp.float32)
        .reshape(case_width, pan_dev)
        .astype(jnp.bfloat16)
    )
    geometry = jnp.concatenate([panel_coords, panel_areas[None, :]], axis=0)
    source_vel, source_geometry = (
        lax.all_gather(vel_t.astype(jnp.float32), ("tgt", "sec"), axis=1, tiled=True).astype(
            vel_t.dtype
        ),
        lax.all_gather(geometry, ("tgt", "sec"), axis=1, tiled=True),
    )
    empty = jnp.zeros((pan_dev, case_width), jnp.float32)
    piece_vel = lax.all_gather(source_vel.astype(jnp.float32), "blk", axis=1, tiled=True).astype(
        jnp.bfloat16
    )
    piece_geometry = lax.all_gather(source_geometry, "blk", axis=1, tiled=True)
    block_span = math.gcd(piece_vel.shape[1], 4096)
    turns = piece_vel.shape[1] // block_span

    def advance(block_index, partial_value):
        vel_block = lax.dynamic_slice_in_dim(piece_vel, block_index * block_span, block_span, 1)
        geo_block = lax.dynamic_slice_in_dim(
            piece_geometry, block_index * block_span, block_span, 1
        )
        return partial_value + pressure_block(geometry, geo_block, vel_block, total_panels)

    pressure_f = lax.fori_loop(0, turns, advance, empty)
    pressure = pressure_f.astype(jnp.bfloat16)
    weighted = (panel_areas[:, None] * pressure.astype(jnp.float32)).astype(jnp.bfloat16)
    contrib = jnp.einsum(
        "bpkm,bpc->bkmc",
        shaped,
        weighted.reshape(block_count, -1, case_width),
        preferred_element_type=jnp.float32,
    )
    onehot = (
        coupling[:, :, None] == jnp.arange(blocks.shape[0], dtype=jnp.int32)[None, None, :]
    ).astype(jnp.float32)
    partial_loads = jnp.einsum(
        "bkj,bkmc->jmc", onehot, contrib, precision=lax.Precision.HIGHEST
    ).reshape(-1, case_width)
    new_loads = lax.psum_scatter(
        partial_loads, ("blk", "tgt", "sec"), scatter_dimension=0, tiled=True
    )
    return (new_loads, pressure)


def solution(mesh):
    in_specs = (
        P("blk", None),
        P(None, ("tgt", "sec"), "blk"),
        P(("blk", "tgt", "sec"), None, None),
        P(("blk", "tgt", "sec"), None),
        P(None, ("blk", "tgt", "sec")),
        P(("blk", "tgt", "sec")),
    )
    out_specs = (P(("blk", "tgt", "sec"), None), P(("blk", "tgt", "sec"), None))
    return jax.shard_map(
        on_device, mesh=mesh, in_specs=in_specs, out_specs=out_specs, check_vma=False
    )
```

profile of v0, /device:TPU:127, one launch (start us, length us, event | category | flops | bytes accessed | tf_op | source)
XLA Modules:
  0.0 1695.3 jit_solution(13466813564859421563)
XLA Ops:
  7.2 0.0 copy-start
  7.2 0.0 copy-start.1
  7.2 0.0 all-gather.3.cloned.1.call-start
  7.2 0.9 copy-done
  8.1 1.1 fusion.18
  9.2 45.5 %all-reduce.1 = bf16[256,128]{0,1:T(8,128)(2,1)} all-reduce(f32[256,128]{0,1:T(8,128)S(1)} %pad_maximum_fusion), channel_id=1, replica_groups=mesh['blk'=16,'tgt'=4,'sec'=4] {'blk'}, use_global_device_ids=true, to_apply=%region_0.0 | all-reduce | flops 32768 | bytes 196608 | tf_op jit(solution)/shard_map/psum | solution.py:58
  54.8 0.0 all-gather.3.cloned.1.call-update
  54.8 0.0 all-gather.5.cloned.1.call-start
  54.8 0.7 fusion.17
  55.5 0.0 copy-start.2
  55.5 0.0 copy-start.4
  55.5 65.5 %all-gather.3.cloned.1.call-done = bf16[4096,128]{0,1:T(8,128)(2,1)} async-done(((bf16[256,128]{0,1:T(8,128)(2,1)}), bf16[4096,128]{0,1:T(8,128)(2,1)}) %all-gather.3.cloned.1.call-update) | async-done | bytes 1048592 | tf_op jit(solution)/shard_map/all_gather | solution.py:59
  121.1 1.6 copy.17
  122.7 0.6 gather_fusion
  123.3 0.0 copy-done.1
  123.3 0.3 fusion.8
  123.6 36.7 %all_gather.18 = bf16[128,2048]{1,0:T(8,128)(2,1)} all-gather(bf16[128,128]{1,0:T(8,128)(2,1)S(1)} %fusion.8), channel_id=1, replica_groups=mesh['blk'=16,'tgt'=4,'sec'=4] {'tgt','sec'}, dimensions={1}, use_global_device_ids=true | all-gather | bytes 557056 | tf_op jit(solution)/shard_map/all_gather | solution.py:72
  160.3 0.0 all-gather.5.cloned.1.call-update
  160.3 0.0 reduce-scatter.2.cloned.1.call-start
  160.4 0.2 copy.16
  160.6 0.0 copy-done.2
  160.6 0.0 copy-done.4
  160.7 34.4 %all_gather.15 = f32[4,2048]{1,0:T(4,128)S(1)} all-gather(f32[4,128]{1,0:T(4,128)S(1)} %pad_maximum_fusion.1), channel_id=1, replica_groups=mesh['blk'=16,'tgt'=4,'sec'=4] {'tgt','sec'}, dimensions={1}, use_global_device_ids=true | all-gather | bytes 34816 | tf_op jit(solution)/shard_map/all_gather | solution.py:75
  195.1 33.2 %all_gather.16 = f32[4,32768]{1,0:T(4,128)S(1)} all-gather(f32[4,2048]{1,0:T(4,128)S(1)} %all_gather.15), channel_id=1, replica_groups=mesh['blk'=16,'tgt'=4,'sec'=4] {'blk'}, dimensions={1}, use_global_device_ids=true | all-gather | bytes 557056 | tf_op jit(solution)/shard_map/all_gather | solution.py:81
  228.3 39.8 %all-gather.5.cloned.1.call-done = bf16[128,32768]{1,0:T(8,128)(2,1)} async-done(((bf16[128,2048]{1,0:T(8,128)(2,1)}), bf16[128,32768]{1,0:T(8,128)(2,1)}) %all-gather.5.cloned.1.call-update) | async-done | bytes 8388624 | tf_op jit(solution)/shard_map/all_gather | solution.py:78
  268.2 92.6 %while.14 = (s32[]{:T(128)}, f32[128,128]{0,1:T(8,128)S(1)}, f32[3,128]{1,0:T(4,128)S(1)}, f32[4,32768]{1,0:T(4,128)S(1)}, bf16[128,32768]{1,0:T(8,128)(2,1)}, /...) while((s32[]{:T(128)}, f32[128,128]{0,1:T(8,128)S(1)}, ...), condition=%wide.region_2.0_spmd.clone, body=%wide.region_1.0_spmd.clone.sunk | while | flops 281088000 | bytes 6001381 | solution.py:92
  268.2 0.2 constant_dynamic-slice_fusion.2
  268.4 9.2 multiply_convert_fusion.4
  277.6 2.1 fusion.29
  279.8 0.2 constant_dynamic-slice_fusion.2
  280.0 9.2 multiply_convert_fusion.4
  289.2 2.1 fusion.29
  291.3 0.2 constant_dynamic-slice_fusion.2
  291.5 9.2 multiply_convert_fusion.4
  300.7 2.1 fusion.29
  302.9 0.2 constant_dynamic-slice_fusion.2
  303.1 9.2 multiply_convert_fusion.4
  312.3 2.1 fusion.29
  314.5 0.2 constant_dynamic-slice_fusion.2
  314.7 9.2 multiply_convert_fusion.4
  323.9 2.1 fusion.29
  326.1 0.2 constant_dynamic-slice_fusion.2
  326.3 9.2 multiply_convert_fusion.4
  335.5 2.1 fusion.29
  337.7 0.2 constant_dynamic-slice_fusion.2
  337.8 9.2 multiply_convert_fusion.4
  347.1 2.1 fusion.29
  349.2 0.2 constant_dynamic-slice_fusion.2
  349.4 9.2 multiply_convert_fusion.4
  358.6 2.1 fusion.29
  360.8 0.0 copy-start.5
  360.8 0.1 copy.13
  360.9 0.0 copy-start.3
  360.9 0.3 convolution_bitcast_fusion
  361.2 0.2 copy-done.5
  361.5 1.1 fusion.14
  362.6 0.0 copy-done.3
  362.6 2.6 copy.14
  365.2 0.0 reduce-scatter.2.cloned.1.call-update
  365.2 1323.6 %reduce-scatter.2.cloned.1.call-done = f32[16,128]{1,0:T(8,128)} async-done(((f32[4096,128]{1,0:T(8,128)}), f32[16,128]{1,0:T(8,128)}) %reduce-scatter.2.cloned.1.call-update) | async-done | bytes 8208 | tf_op jit(solution)/shard_map/reduce_scatter | solution.py:107
  (29 shorter events, 0.3 us)
Async XLA Ops:
  7.2 1.0 copy-start
  7.2 116.1 %copy-start.1 = (bf16[128,8,128]{2,1,0:T(8,128)(2,1)S(1)}, bf16[128,8,128]{2,1,0:T(8,128)(2,1)}, u32[]{:S(2)}) copy-start(bf16[128,8,128]{2,1,0:T(8,128)(2,1)} %param.10) | copy-start | bytes 786436
  7.2 113.9 %all-gather.3.cloned.1.call-start = ((), (), s32[]{:S(2)}) async-start(), calls=%async_computation.1 | async-start | bytes 1114112 | tf_op jit(solution)/shard_map/all_gather | solution.py:59
  54.8 213.4 %all-gather.5.cloned.1.call-start = ((), (), s32[]{:S(2)}) async-start(), calls=%async_computation.2 | async-start | bytes 8912896 | tf_op jit(solution)/shard_map/all_gather | solution.py:78
  55.5 105.1 %copy-start.2 = (f32[3,128]{1,0:T(4,128)S(1)}, f32[3,128]{1,0:T(4,128)}, u32[]{:S(2)}) copy-start(f32[3,128]{1,0:T(4,128)} %param.12) | copy-start | bytes 4612
  55.5 105.1 %copy-start.4 = (f32[128]{0:T(128)S(1)}, f32[128]{0:T(128)}, u32[]{:S(2)}) copy-start(f32[128]{0:T(128)} %param.13) | copy-start | bytes 1540
  160.3 1528.4 %reduce-scatter.2.cloned.1.call-start = ((), (), s32[]{:S(2)}) async-start(), calls=%async_computation.3 | async-start | bytes 2105344 | tf_op jit(solution)/shard_map/reduce_scatter | solution.py:107
  360.8 0.7 copy-start.5
  360.9 1.7 copy-start.3
Sparse Core Ops, SparseCore 0:
  54.9 66.0 all-gather.2
  160.4 107.7 all-gather.4
  365.3 1323.4 reduce-scatter.1
where the time goes:
time: 1700 us
  waiting for transfers between devices  1430 us (84%)
  blocking collectives  150 us (9%)
  other arithmetic  76 us (4%)
  matrix products  19.6 us (1%)
    reduce_scatter x1, waiting for transfers between devices, on_device(): lax.psum_scatter(partial_loads, ('blk', 'tgt', 'sec'), scatter_dimension=...  1320 us
    convert_element_type x8, other arithmetic, pressure_block(): (jnp.cos(phase_angle) * weight).astype(jnp.bfloat16)  73.6 us
    all_gather x1, waiting for transfers between devices, on_device(): lax.all_gather(modal_sum.astype(jnp.bfloat16), ('tgt', 'sec'), axis=0, ti...  65.5 us
    psum x1, blocking collectives, on_device(): modal_sum = lax.psum(modal_sum, 'blk')  45.5 us
    all_gather x1, waiting for transfers between devices, on_device(): lax.all_gather(source_vel.astype(jnp.float32), 'blk', axis=1, tiled=True)  39.8 us
    all_gather x1, blocking collectives, on_device(): lax.all_gather(vel_t.astype(jnp.float32), ('tgt', 'sec'), axis=1, tiled=T...  36.7 us
    all_gather x1, blocking collectives, on_device(): lax.all_gather(geometry, ('tgt', 'sec'), axis=1, tiled=True)  34.4 us
  transfers between devices with their start and end apart: 3, of which 3 were waited for; matrix products, arithmetic and copies ran while one was open for 0% of the time, Pallas kernels for 0%

commit v1 on v0

v1 whole, which is shorter than its diff:
```python
import functools
import math

import jax
import jax.numpy as jnp
from jax import lax
from jax.experimental import pallas as pl
from jax.experimental.pallas import tpu as pltpu
from jax.sharding import PartitionSpec as P

MESH = pl.DeviceIdType.MESH
F32 = jnp.float32
BF16 = jnp.bfloat16

WAVE = 40.0
YL = 2
PB = 128
CW = 128
RW = 16
ROWS = 64

SIN = (4.442879567546083, -7.307816684491776, 3.5977741780871795, -0.7911993921612632)
COS = (1.4142040148090755, -6.977637323456285, 5.715187874756681, -1.7282138922234693)

GEO_S, GEO_T, RS_AMP, AG_Z, AG_XY, AG_C, RS_PC, RS_PZ, RS_LC, RS_LXY, RS_LZ = range(11)


def horner(coefs, u):
    acc = u * coefs[-1] + coefs[-2]
    for value in coefs[-3::-1]:
        acc = acc * u + value
    return acc


def turn_rows(value):
    n = value.shape[1]
    return jnp.transpose(jnp.broadcast_to(value, (n, n)))


def rotated(value):
    half = value.shape[1] // 2
    turned = pltpu.roll(value, half, 1)
    lane = lax.broadcasted_iota(jnp.int32, value.shape, 1)
    return jnp.where(lane < half, -turned, turned)


def kernel(
    dims,
    loads_ref,
    rec_ref,
    shp_ref,
    cpl_ref,
    crd_ref,
    area_ref,
    out_ref,
    prs_ref,
    geo_s,
    geo_t,
    tgt_b,
    area_b,
    kmat,
    acc,
    part,
    part_h,
    amp_in,
    amp,
    vels,
    w_ref,
    p_out,
    pc_in,
    pz_in,
    shp_t,
    inv,
    cbuf,
    lc_out,
    lc_in,
    lx_out,
    lx_in,
    lx_own,
    lz_out,
    lz_in,
    send_sem,
    recv_sem,
    vsend_sem,
    vrecv_sem,
):
    X, YH, Z, KB = dims
    Y = YH * YL
    n_xy, n_zc, n_blk = X * Y, 2 * Z, YL * Z
    mb = Z * RW
    total_panels = float(PB * 2 * X * Y * Z)

    blk, tgt, sec = lax.axis_index("blk"), lax.axis_index("tgt"), lax.axis_index("sec")
    yl, z = lax.div(blk, Z), lax.rem(blk, Z)
    yh, core = lax.div(tgt, 2), lax.rem(tgt, 2)
    x = sec
    y = yh * YL + yl

    def device(x_, y_, z_, c_):
        return (lax.rem(y_, YL) * Z + z_, lax.div(y_, YL) * 2 + c_, x_)

    def shifted(dx=0, dy=0, dz=0, dc=0):
        return (
            lax.rem(x + dx, X),
            lax.rem(y + dy, Y),
            lax.rem(z + dz, Z),
            lax.rem(core + dc, 2),
        )

    def near(d, n):
        return min(d, n - d)

    xy_steps = sorted(range(1, n_xy), key=lambda q: near(q % X, X) + near(q // X, Y))
    z_steps = sorted(range(1, Z), key=lambda q: near(q, Z))
    zc_steps = [dc * Z + dz for dc in range(2) for dz in range(Z) if dc or dz]
    blk_steps = [dl * Z + dz for dl in range(YL) for dz in range(Z) if dl or dz]

    def yl_place(dl, dz):
        y_ = yh * YL + lax.rem(yl + dl, YL)
        return (x, y_, lax.rem(z + dz, Z), core)

    def send(phase, src, dst, place, send_s=None, recv_s=None):
        copy = pltpu.make_async_remote_copy(
            src_ref=src,
            dst_ref=dst,
            send_sem=send_sem.at[phase] if send_s is None else send_s,
            recv_sem=recv_sem.at[phase] if recv_s is None else recv_s,
            device_id=device(*place),
            device_id_type=MESH,
        )
        copy.start()
        return copy

    def wait_bytes(sem, ref):
        pltpu.make_async_copy(ref, ref, sem).wait()

    barrier = pltpu.get_barrier_semaphore()
    places = [shifted(dx=q % X, dy=q // X) for q in xy_steps]
    places += [shifted(dz=q % Z, dc=q // Z) for q in zc_steps]
    places += [yl_place(q // Z, q % Z) for q in blk_steps if q // Z]
    for place in places:
        pl.semaphore_signal(barrier, inc=1, device_id=device(*place), device_id_type=MESH)

    half_scale = 0.5 * WAVE / math.pi
    geo_s[0, 0:3, :] = crd_ref[...] * half_scale
    geo_s[0, 3:4, :] = area_ref[...] * (half_scale * half_scale / total_panels)
    geo_s[0, 4:8, :] = jnp.zeros((4, PB), F32)
    geo_t[0, :, :] = geo_s[0, :, :]
    loads = loads_ref[...]
    loads_rot = rotated(loads.astype(F32)).astype(BF16)
    psum = jnp.dot(rec_ref[0], loads, preferred_element_type=F32) + jnp.dot(
        rec_ref[1], loads_rot, preferred_element_type=F32
    )
    part[...] = psum.reshape(n_blk, RW, CW)
    part_h[...] = psum.astype(BF16).reshape(n_blk, RW, CW)

    pl.semaphore_wait(barrier, len(places))

    for q in reversed(xy_steps):
        send(GEO_S, geo_s.at[0], geo_s.at[q], shifted(dx=q % X, dy=q // X))
    for q in zc_steps:
        send(GEO_T, geo_t.at[0], geo_t.at[q], shifted(dz=q % Z, dc=q // Z))
    for q in blk_steps:
        place = yl_place(q // Z, q % Z)
        owner = lax.rem(place[1], YL) * Z + place[2]
        send(RS_AMP, part_h.at[owner], amp_in.at[q - 1], place)

    area_col = turn_rows(area_ref[...])
    area_b[...] = area_col
    for k in range(KB):
        shp_t[k] = jnp.transpose(shp_ref[k].astype(F32)).astype(BF16)

    def fill_inv(j, carry):
        found = jnp.int32(KB)
        for k in range(KB):
            found = jnp.where(cpl_ref[0, k] == j, jnp.int32(k), found)
        inv[j] = found
        return carry

    lax.fori_loop(0, 2 * YH * X * YL, fill_inv, 0)

    def turn_targets(slot):
        rows = pl.ds(slot * PB, PB)
        for axis in range(3):
            tgt_b[axis, rows, :] = turn_rows(geo_t[slot, axis : axis + 1, :])

    wait_bytes(recv_sem.at[GEO_T], geo_t.at[pl.ds(1, n_zc - 1)])

    def turn_step(slot, carry):
        turn_targets(slot)
        return carry

    lax.fori_loop(0, n_zc, turn_step, 0)
    wait_bytes(recv_sem.at[GEO_S], geo_s.at[pl.ds(1, n_xy - 1)])

    steps = n_zc * PB // ROWS

    def kernel_chunks(lo, hi):
        def chunk(d, carry):
            shape = (ROWS, PB)
            sx = jnp.broadcast_to(geo_s[d, 0:1, :], shape)
            sy = jnp.broadcast_to(geo_s[d, 1:2, :], shape)
            sz = jnp.broadcast_to(geo_s[d, 2:3, :], shape)
            sa = jnp.broadcast_to(geo_s[d, 3:4, :], shape)

            def rows_step(i, inner):
                rows = pl.ds(pl.multiple_of(i * ROWS, ROWS), ROWS)
                dx = tgt_b[0, rows, :] - sx
                dy = tgt_b[1, rows, :] - sy
                dz = tgt_b[2, rows, :] - sz
                d2 = dx * dx + dy * dy + dz * dz + sa
                r = lax.rsqrt(d2)
                h = d2 * r
                f = h - jnp.round(h)
                u = f * f
                s = horner(SIN, u) * f
                c = horner(COS, u)
                rs = r * s
                kmat[d, rows, 0:PB] = (r - rs * s).astype(BF16)
                kmat[d, rows, PB : 2 * PB] = (rs * c).astype(BF16)
                return inner

            return lax.fori_loop(0, steps, rows_step, carry)

        lax.fori_loop(lo, hi, chunk, 0)

    cuts = [round(n_xy * part_of / 16) for part_of in (0, 3, 6, 12, 14, 16)]

    kernel_chunks(cuts[0], cuts[1])

    wait_bytes(recv_sem.at[RS_AMP], amp_in)
    asum = part[blk]
    for q in range(n_blk - 1):
        asum = asum + amp_in[q].astype(F32)
    xl = x * YL + yl
    amp[yh, core, xl, z] = asum.astype(BF16)
    for dz in reversed(z_steps):
        mine = amp.at[yh, core, xl, z]
        send(AG_Z, mine, mine, shifted(dz=dz))

    kernel_chunks(cuts[1], cuts[2])
    wait_bytes(recv_sem.at[AG_Z], amp.at[0, 0, 0, pl.ds(0, Z - 1)])
    for q in reversed(xy_steps):
        mine = amp.at[yh, core, xl]
        send(AG_XY, mine, mine, shifted(dx=q % X, dy=q // X))

    kernel_chunks(cuts[2], cuts[3])
    for _ in range(1):
        wait_bytes(recv_sem.at[AG_XY], kmat.at[0, pl.ds(0, (n_xy - 1) * mb * CW // (2 * PB)), :])
    mine = amp.at[:, core]
    send(AG_C, mine, mine, shifted(dc=1))
    kernel_chunks(cuts[3], cuts[4])
    wait_bytes(recv_sem.at[AG_C], mine)

    vel = jnp.zeros((PB, CW), F32)
    for k in range(KB):
        j = cpl_ref[0, k]
        jl = lax.rem(j, X * YL)
        jc = lax.rem(lax.div(j, X * YL), 2)
        jh = lax.div(j, X * YL * 2)
        block = amp[jh, jc, jl].reshape(mb, CW)
        vel = vel + jnp.dot(shp_ref[k], block, preferred_element_type=F32)
    vels[0] = (vel * area_b[...] * (half_scale / math.sqrt(total_panels))).astype(BF16)
    for q in reversed(xy_steps):
        send(
            0,
            vels.at[0],
            vels.at[q],
            shifted(dx=q % X, dy=q // X),
            vsend_sem.at[0],
            vrecv_sem.at[q - 1],
        )
    kernel_chunks(cuts[4], cuts[5])

    mm_rows = min(512, n_zc * PB)

    def add_chunk(q, first):
        value = vels[q]
        w_ref[0:PB, :] = value
        w_ref[PB : 2 * PB, :] = rotated(value.astype(F32)).astype(BF16)

        def mm_step(i, carry):
            rows = pl.ds(pl.multiple_of(i * mm_rows, mm_rows), mm_rows)
            prod = jnp.dot(kmat[q, rows, :], w_ref[...], preferred_element_type=F32)
            acc[rows, :] = prod if first else acc[rows, :] + prod
            return carry

        lax.fori_loop(0, n_zc * PB // mm_rows, mm_step, 0)

    add_chunk(0, True)
    for q in xy_steps:
        wait_bytes(vrecv_sem.at[q - 1], vels.at[q])
        add_chunk(q, False)

    half = Z * PB
    p_out[...] = acc[half : 2 * half, :].astype(BF16).reshape(Z, PB, CW)
    send(RS_PC, p_out, pc_in, shifted(dc=1))
    wait_bytes(recv_sem.at[RS_PC], pc_in)
    wait_bytes(send_sem.at[RS_PC], p_out)
    for dz in reversed(z_steps):
        rows = slice(dz * PB, (dz + 1) * PB)
        p_out[dz] = (acc[rows, :] + pc_in[dz].astype(F32)).astype(BF16)
        send(RS_PZ, p_out.at[dz], pz_in.at[dz - 1], shifted(dz=Z - dz))
    total = acc[0:PB, :] + pc_in[0].astype(F32)
    wait_bytes(recv_sem.at[RS_PZ], pz_in)
    for dz in range(Z - 1):
        total = total + pz_in[dz].astype(F32)
    pressure = total.astype(BF16)
    prs_ref[...] = pressure
    weighted = (area_b[...] * pressure.astype(F32)).astype(BF16)

    for k in range(KB):
        cbuf[k] = (
            jnp.dot(shp_t[k], weighted, preferred_element_type=F32)
            .astype(BF16)
            .reshape(2, X, RW, CW)
        )
    cbuf[KB] = jnp.zeros((2, X, RW, CW), BF16)
    other = 1 - core
    n_j = YL * Z * YH
    for j in range(n_j):
        lc_out[j] = cbuf[inv[j], other]
    send(RS_LC, lc_out, lc_in, shifted(dc=1))
    wait_bytes(recv_sem.at[RS_LC], lc_in)
    wait_bytes(send_sem.at[RS_LC], lc_out)
    for j in range(n_j):
        jl, jz, jh = j // (Z * YH), j // YH % Z, j % YH
        both = cbuf[inv[j], core].astype(F32) + lc_in[j].astype(F32)
        for xx in range(X):
            lx_own[jl, jh, xx, jz] = both[xx]
            lx_out[jl, jh, xx, jz] = both[xx].astype(BF16)
    for q in reversed(xy_steps):
        place = shifted(dx=q % X, dy=q // X)
        src = lx_out.at[lax.rem(place[1], YL), lax.div(place[1], YL), place[0]]
        send(RS_LXY, src, lx_in.at[q - 1], place)
    wait_bytes(recv_sem.at[RS_LXY], lx_in)
    lsum = lx_own[yl, yh, x]
    for q in range(n_xy - 1):
        lsum = lsum + lx_in[q].astype(F32)
    lx_own[yl, yh, x] = lsum
    lz_out[...] = lsum.astype(BF16)
    for dz in reversed(z_steps):
        place = shifted(dz=dz)
        send(RS_LZ, lz_out.at[place[2]], lz_in.at[dz - 1], place)
    fin = lx_own[yl, yh, x, z]
    wait_bytes(recv_sem.at[RS_LZ], lz_in)
    for dz in range(Z - 1):
        fin = fin + lz_in[dz].astype(F32)
    out_ref[...] = fin

    wait_bytes(send_sem.at[GEO_S], geo_s.at[pl.ds(1, n_xy - 1)])
    wait_bytes(send_sem.at[GEO_T], geo_t.at[pl.ds(1, n_zc - 1)])
    wait_bytes(send_sem.at[RS_AMP], amp_in)
    wait_bytes(send_sem.at[AG_Z], amp.at[0, 0, 0, pl.ds(0, Z - 1)])
    wait_bytes(send_sem.at[AG_XY], kmat.at[0, pl.ds(0, (n_xy - 1) * mb * CW // (2 * PB)), :])
    wait_bytes(send_sem.at[AG_C], mine)
    wait_bytes(vsend_sem.at[0], vels.at[pl.ds(1, n_xy - 1)])
    wait_bytes(send_sem.at[RS_PZ], pz_in)
    wait_bytes(send_sem.at[RS_LXY], lx_in)
    wait_bytes(send_sem.at[RS_LZ], lz_in)


def solution(mesh):
    Z = mesh.shape["blk"] // YL
    YH = mesh.shape["tgt"] // 2
    X = mesh.shape["sec"]
    Y = YH * YL
    n_xy, n_zc, n_blk = X * Y, 2 * Z, YL * Z
    mb = Z * RW

    def on_device(modal_loads, receptance, shapes, coupling, panel_coords, panel_areas):
        KB = shapes.shape[1]
        dma = pltpu.SemaphoreType.DMA
        scratch = [
            pltpu.VMEM((n_xy, 8, PB), F32),
            pltpu.VMEM((n_zc, 8, PB), F32),
            pltpu.VMEM((3, n_zc * PB, PB), F32),
            pltpu.VMEM((PB, PB), F32),
            pltpu.VMEM((n_xy, n_zc * PB, 2 * PB), BF16),
            pltpu.VMEM((n_zc * PB, CW), F32),
            pltpu.VMEM((n_blk, RW, CW), F32),
            pltpu.VMEM((n_blk, RW, CW), BF16),
            pltpu.VMEM((n_blk - 1, RW, CW), BF16),
            pltpu.VMEM((YH, 2, X * YL, Z, RW, CW), BF16),
            pltpu.VMEM((n_xy, PB, CW), BF16),
            pltpu.VMEM((2 * PB, CW), BF16),
            pltpu.VMEM((Z, PB, CW), BF16),
            pltpu.VMEM((Z, PB, CW), BF16),
            pltpu.VMEM((Z - 1, PB, CW), BF16),
            pltpu.VMEM((KB, mb, PB), BF16),
            pltpu.SMEM((n_blk * YH,), jnp.int32),
            pltpu.VMEM((KB + 1, 2, X, RW, CW), BF16),
            pltpu.VMEM((n_blk * YH, X, RW, CW), BF16),
            pltpu.VMEM((n_blk * YH, X, RW, CW), BF16),
            pltpu.VMEM((YL, YH, X, Z, RW, CW), BF16),
            pltpu.VMEM((n_xy - 1, Z, RW, CW), BF16),
            pltpu.VMEM((YL, YH, X, Z, RW, CW), F32),
            pltpu.VMEM((Z, RW, CW), BF16),
            pltpu.VMEM((Z - 1, RW, CW), BF16),
            dma((11,)),
            dma((11,)),
            dma((1,)),
            dma((n_xy - 1,)),
        ]
        vmem = pl.BlockSpec(memory_space=pltpu.VMEM)
        new_loads, pressure = pl.pallas_call(
            functools.partial(kernel, (X, YH, Z, KB)),
            out_shape=(
                jax.ShapeDtypeStruct((RW, CW), F32),
                jax.ShapeDtypeStruct((PB, CW), BF16),
            ),
            in_specs=[vmem, vmem, vmem, pl.BlockSpec(memory_space=pltpu.SMEM), vmem, vmem],
            out_specs=(vmem, vmem),
            scratch_shapes=scratch,
            compiler_params=pltpu.CompilerParams(
                collective_id=0,
                has_side_effects=True,
                vmem_limit_bytes=58 * 1024 * 1024,
            ),
        )(
            modal_loads,
            receptance,
            jnp.transpose(shapes, (1, 0, 2)),
            coupling,
            panel_coords,
            panel_areas.reshape(1, PB),
        )
        return new_loads, pressure

    owned = ("blk", "tgt", "sec")
    in_specs = (
        P("blk", None),
        P(None, ("tgt", "sec"), "blk"),
        P(owned, None, None),
        P(owned, None),
        P(None, owned),
        P(owned),
    )
    return jax.shard_map(
        on_device,
        mesh=mesh,
        in_specs=in_specs,
        out_specs=(P(owned, None), P(owned, None)),
        check_vma=False,
    )
```

time: 1700 us -> 93.7 us (0.06)
  the two profiles are of different devices: /device:TPU:127 before, /device:TPU:1 now
where the time goes in v1:
time: 93.7 us; the launch traced here: 93.5 us
  Pallas kernels  88.5 us (94%)
  local copies, waits for them, and re-layouts  4.35 us (5%)
    pallas_call x1, Pallas kernels, on_device(): pl.pallas_call(functools.partial(kernel, (X, YH, Z, KB)), out_shape=(jax....  88.5 us
    unnamed x3, local copies, waits for them, and re-layouts  4.35 us

profile of v1, /device:TPU:1, one launch (start us, length us, event | category | flops | bytes accessed | tf_op | source)
XLA Modules:
  0.0 93.5 jit_solution(13466803809459326835)
XLA Ops:
  0.6 1.7 %copy.10 = bf16[128,8,128]{2,0,1:T(8,128)(2,1)} copy(bf16[128,8,128]{2,1,0:T(8,128)(2,1)} %param.8) | data formatting | bytes 524288 | tf_op args[2]
  2.3 88.5 %shard_map.77 = (f32[16,128]{1,0:T(8,128)}, bf16[128,128]{1,0:T(8,128)(2,1)}) custom-call(bf16[256,128]{1,0:T(8,128)(2,1)} %loads_ref.1, bf16[2,256,256]{2,1,0:T(8,128)(2,1)} %rec_ref.1, bf16[8,128,128]{2,1,0:T(8,128)(2,1)} %bitcast.4, s32[1,8]{1,0:T(1,128)} %cpl_ref.1, f32[3,128]{1,0:T(4,128)} %crd_ref.1, f32[1,128]{1,0:T(1,128)} %bitcast.5), custom_call_target="tpu_custom_call" | custom-call | tf_op jit(solution)/shard_map/pallas_call | solution.py:406
  90.8 1.3 %copy.13 = f32[16,128]{1,0:T(8,128)} copy(f32[16,128]{1,0:T(8,128)} %get-tuple-element.4) | data formatting | bytes 16384
  92.1 1.4 %copy.14 = bf16[128,128]{1,0:T(8,128)(2,1)} copy(bf16[128,128]{1,0:T(8,128)(2,1)} %get-tuple-element.5) | data formatting | bytes 65536

commit v2 on v1

v2 whole, which is shorter than its diff:
```python
import functools
import math

import jax
import jax.numpy as jnp
from jax import lax
from jax.experimental import pallas as pl
from jax.experimental.pallas import tpu as pltpu
from jax.sharding import PartitionSpec as P

MESH = pl.DeviceIdType.MESH
F32 = jnp.float32
BF16 = jnp.bfloat16

WAVE = 40.0
YL = 2
PB = 128
CW = 128
RW = 16
ROWS = 128

CUTS = (0, 3, 5, 7, 9, 11, 12, 14)

SIN = (4.442879567546083, -7.307816684491776, 3.5977741780871795, -0.7911993921612632)
COS = (1.4142040148090755, -6.977637323456285, 5.715187874756681, -1.7282138922234693)

GEO_S, GEO_T, RS_AMP, AG_Z, AG_C, RS_PZ, RS_LXY, RS_LZ, AG_XY, VEL, RS_PC, RS_LC, N_SEM = (
    0, 1, 2, 3, 4, 5, 6, 7, 8, 12, 16, 20, 24,
)


def horner(coefs, u):
    acc = u * coefs[-1] + coefs[-2]
    for value in coefs[-3::-1]:
        acc = acc * u + value
    return acc


def turn_rows(value):
    n = value.shape[1]
    return jnp.transpose(jnp.broadcast_to(value, (n, n)))


def rotated(value):
    half = value.shape[1] // 2
    turned = pltpu.roll(value, half, 1)
    lane = lax.broadcasted_iota(jnp.int32, value.shape, 1)
    return jnp.where(lane < half, -turned, turned)


def near(d, n):
    return min(d, n - d)


def kernel(
    dims,
    loads_ref,
    rec_ref,
    shp_ref,
    cpl_ref,
    crd_ref,
    area_ref,
    out_ref,
    prs_ref,
    geo_s,
    geo_t,
    tgt_b,
    area_b,
    kmat,
    acc,
    part,
    part_h,
    amp_in,
    amp,
    vels,
    w_ref,
    p_out,
    pc_in,
    pz_out,
    pz_in,
    shp_f,
    shp_k,
    shp_t,
    inv,
    cbuf,
    lc_out,
    lc_in,
    lx_out,
    lx_in,
    lx_own,
    lz_out,
    lz_in,
    send_sem,
    recv_sem,
):
    X, YH, Z, KB = dims
    Y = YH * YL
    n_xy, n_zc, n_blk = X * Y, 2 * Z, YL * Z
    mb = Z * RW
    total_panels = float(PB * 2 * X * Y * Z)

    blk, tgt, sec = lax.axis_index("blk"), lax.axis_index("tgt"), lax.axis_index("sec")
    yl, z = lax.div(blk, Z), lax.rem(blk, Z)
    yh, core = lax.div(tgt, 2), lax.rem(tgt, 2)
    x = sec
    y = yh * YL + yl

    def device(x_, y_, z_, c_):
        return (lax.rem(y_, YL) * Z + z_, lax.div(y_, YL) * 2 + c_, x_)

    def shifted(dx=0, dy=0, dz=0, dc=0):
        return (
            lax.rem(x + dx, X),
            lax.rem(y + dy, Y),
            lax.rem(z + dz, Z),
            lax.rem(core + dc, 2),
        )

    xy_steps = sorted(((q % X, q // X) for q in range(n_xy)), key=lambda s: near(s[0], X) + near(s[1], Y))
    z_steps = sorted(range(Z), key=lambda q: -near(q, Z))
    zc_steps = [(dc, dz) for dc in (1, 0) for dz in z_steps]
    y_steps = sorted(range(Y), key=lambda q: -near(q, Y))
    blk_steps = sorted(
        ((dl, dz) for dl in range(YL) for dz in range(Z) if dl or dz), key=lambda s: -s[0] - near(s[1], Z)
    )
    groups = [range(n_xy * g // 4, n_xy * (g + 1) // 4) for g in range(4)]

    def yl_place(dl, dz):
        y_ = yh * YL + lax.rem(yl + dl, YL)
        return (x, y_, lax.rem(z + dz, Z), core)

    def send(send_s, recv_s, src, dst, place):
        pltpu.make_async_remote_copy(
            src_ref=src,
            dst_ref=dst,
            send_sem=send_sem.at[send_s],
            recv_sem=recv_sem.at[recv_s],
            device_id=device(*place),
            device_id_type=MESH,
        ).start()

    def wait_bytes(sem, ref):
        pltpu.make_async_copy(ref, ref, sem).wait()

    unfinished = []

    def finish():
        for phase, ref in unfinished:
            wait_bytes(send_sem.at[phase], ref)

    barrier = pltpu.get_barrier_semaphore()
    places = [shifted(dx=dx, dy=dy) for dx, dy in reversed(xy_steps[1:])]
    places += [shifted(dz=dz, dc=dc) for dc, dz in zc_steps[:-1]]
    places += [yl_place(dl, dz) for dl, dz in blk_steps if dl and dz]
    for place in places:
        pl.semaphore_signal(barrier, inc=1, device_id=device(*place), device_id_type=MESH)

    half_scale = 0.5 * WAVE / math.pi
    geo_s[0, 0:3, :] = crd_ref[...] * half_scale
    geo_s[0, 3:4, :] = area_ref[...] * (half_scale * half_scale / total_panels)
    geo_s[0, 4:8, :] = jnp.zeros((4, PB), F32)
    geo_t[n_zc - 1, :, :] = geo_s[0, :, :]
    loads = loads_ref[...]
    loads_rot = rotated(loads.astype(F32)).astype(BF16)
    psum = jnp.dot(rec_ref[0], loads, preferred_element_type=F32) + jnp.dot(
        rec_ref[1], loads_rot, preferred_element_type=F32
    )
    part[...] = psum.reshape(n_blk, RW, CW)
    part_h[...] = psum.astype(BF16).reshape(n_blk, RW, CW)

    pl.semaphore_wait(barrier, len(places))

    for q, (dl, dz) in enumerate(blk_steps):
        place = yl_place(dl, dz)
        owner = lax.rem(place[1], YL) * Z + place[2]
        send(RS_AMP, RS_AMP, part_h.at[owner], amp_in.at[q], place)
    for n in range(1, n_xy):
        dx, dy = xy_steps[n]
        send(GEO_S, GEO_S, geo_s.at[0], geo_s.at[n], shifted(dx=dx, dy=dy))
    for t in range(n_zc - 1):
        dc, dz = zc_steps[t]
        send(GEO_T, GEO_T, geo_t.at[n_zc - 1], geo_t.at[t], shifted(dz=dz, dc=dc))
    unfinished.append((GEO_S, geo_s.at[pl.ds(1, n_xy - 1)]))
    unfinished.append((GEO_T, geo_t.at[pl.ds(1, n_zc - 1)]))
    unfinished.append((RS_AMP, amp_in))

    area_b[...] = turn_rows(area_ref[...])
    shp_f[...] = shp_ref[...].astype(F32).reshape(PB * KB, mb)
    for k in range(KB):
        block = shp_f[pl.ds(k, PB, stride=KB), :]
        shp_k[k] = block.astype(BF16)
        shp_t[k] = jnp.transpose(block).astype(BF16)
    cbuf[KB] = jnp.zeros((2, X, RW, CW), BF16)

    def fill_inv(j, carry):
        found = jnp.int32(KB)
        for k in range(KB):
            found = jnp.where(cpl_ref[0, k] == j, jnp.int32(k), found)
        inv[j] = found
        return carry

    lax.fori_loop(0, n_blk * YH, fill_inv, 0)

    wait_bytes(recv_sem.at[GEO_T], geo_t.at[pl.ds(1, n_zc - 1)])

    def turn_step(slot, carry):
        rows = pl.ds(pl.multiple_of(slot * PB, PB), PB)
        for axis in range(3):
            tgt_b[axis, rows, :] = turn_rows(geo_t[slot, axis : axis + 1, :])
        return carry

    lax.fori_loop(0, n_zc, turn_step, 0)
    wait_bytes(recv_sem.at[GEO_S], geo_s.at[pl.ds(1, n_xy - 1)])

    steps = n_zc * PB // ROWS

    def kernel_chunks(lo, hi):
        def chunk(d, carry):
            shape = (ROWS, PB)
            sx = jnp.broadcast_to(geo_s[d, 0:1, :], shape)
            sy = jnp.broadcast_to(geo_s[d, 1:2, :], shape)
            sz = jnp.broadcast_to(geo_s[d, 2:3, :], shape)
            sa = jnp.broadcast_to(geo_s[d, 3:4, :], shape)

            def rows_step(i, inner):
                rows = pl.ds(pl.multiple_of(i * ROWS, ROWS), ROWS)
                dx = tgt_b[0, rows, :] - sx
                dy = tgt_b[1, rows, :] - sy
                dz = tgt_b[2, rows, :] - sz
                d2 = dx * dx + dy * dy + dz * dz + sa
                r = lax.rsqrt(d2)
                h = d2 * r
                f = h - jnp.round(h)
                u = f * f
                s = horner(SIN, u) * f
                c = horner(COS, u)
                rs = r * s
                kmat[d, rows, 0:PB] = (r - rs * s).astype(BF16)
                kmat[d, rows, PB : 2 * PB] = (rs * c).astype(BF16)
                return inner

            return lax.fori_loop(0, steps, rows_step, carry)

        lax.fori_loop(lo, hi, chunk, 0)

    cuts = [round(n_xy * part_of / 16) for part_of in CUTS]

    kernel_chunks(cuts[0], cuts[1])

    wait_bytes(recv_sem.at[RS_AMP], amp_in)
    asum = part[blk]
    for q in range(n_blk - 1):
        asum = asum + amp_in[q].astype(F32)
    xl = x * YL + yl
    amp[yh, core, xl, z] = asum.astype(BF16)
    for dz in z_steps[:-1]:
        mine = amp.at[yh, core, xl, z]
        send(AG_Z, AG_Z, mine, mine, shifted(dz=dz))
    seven = amp.at[0, 0, 0, pl.ds(0, Z - 1)]
    unfinished.append((AG_Z, seven))

    kernel_chunks(cuts[1], cuts[2])
    wait_bytes(recv_sem.at[AG_Z], seven)
    mine = amp.at[yh, core, xl]
    for g, group in enumerate(groups):
        for n in group:
            dx, dy = xy_steps[n]
            if n:
                send(AG_XY, AG_XY + g, mine, mine, shifted(dx=dx, dy=dy))
    unfinished.append((AG_XY, vels.at[pl.ds(1, n_xy - 1), pl.ds(0, mb)]))
    send(AG_C, AG_C, mine, mine, shifted(dc=1))

    for g, group in enumerate(groups):
        kernel_chunks(cuts[2 + g], cuts[3 + g])
        rest = [n for n in group if n]
        if not rest:
            continue
        wait_bytes(recv_sem.at[AG_XY + g], vels.at[pl.ds(1, len(rest)), pl.ds(0, mb)])
        for n in rest:
            dx, dy = xy_steps[n]
            sx, sy = lax.rem(x + X - dx, X), lax.rem(y + Y - dy, Y)
            theirs = amp.at[lax.div(sy, YL), core, sx * YL + lax.rem(sy, YL)]
            send(AG_C, AG_C, theirs, theirs, shifted(dc=1))
    half_amp = amp.at[:, 0]
    unfinished.append((AG_C, half_amp))
    kernel_chunks(cuts[6], cuts[7])
    wait_bytes(recv_sem.at[AG_C], half_amp)

    vel = jnp.zeros((PB, CW), F32)
    for k in range(KB):
        j = cpl_ref[0, k]
        jl = lax.rem(j, X * YL)
        jc = lax.rem(lax.div(j, X * YL), 2)
        jh = lax.div(j, X * YL * 2)
        block = amp[jh, jc, jl].reshape(mb, CW)
        vel = vel + jnp.dot(shp_k[k], block, preferred_element_type=F32)
    vels[0] = (vel * area_b[...] * (half_scale / math.sqrt(total_panels))).astype(BF16)
    for g, group in enumerate(groups):
        for n in group:
            dx, dy = xy_steps[n]
            if n:
                send(VEL, VEL + g, vels.at[0], vels.at[n], shifted(dx=dx, dy=dy))
    unfinished.append((VEL, vels.at[pl.ds(1, n_xy - 1)]))
    kernel_chunks(cuts[7], n_xy)

    def weights(g):
        group = groups[g]
        rest = [n for n in group if n]
        if rest:
            wait_bytes(recv_sem.at[VEL + g], vels.at[pl.ds(rest[0], len(rest))])
        for n in group:
            value = vels[n]
            w_ref[n, 0:PB, :] = value
            w_ref[n, PB : 2 * PB, :] = rotated(value.astype(F32)).astype(BF16)

    def products(g, rows):
        total = None
        for n in groups[g]:
            term = jnp.dot(kmat[n, rows, :], w_ref[n], preferred_element_type=F32)
            total = term if total is None else total + term
        return total

    mm_rows = min(512, n_zc * PB)
    for g in range(3):
        weights(g)

        def mm_step(i, carry):
            rows = pl.ds(pl.multiple_of(i * mm_rows, mm_rows), mm_rows)
            prod = products(g, rows)
            acc[rows, :] = prod if g == 0 else acc[rows, :] + prod
            return carry

        lax.fori_loop(0, n_zc * PB // mm_rows, mm_step, 0)

    weights(3)
    pair = 2
    n_pair = Z // pair
    for i in range(n_pair):
        rows = slice(i * pair * PB, (i + 1) * pair * PB)
        value = acc[rows, :] + products(3, rows)
        p_out[i] = value.astype(BF16).reshape(pair, PB, CW)
        send(RS_PC, RS_PC + i, p_out.at[i], pc_in.at[i], shifted(dc=1))
    unfinished.append((RS_PC, p_out))
    total = None
    for i in range(n_pair):
        rows = slice((n_pair + i) * pair * PB, (n_pair + i + 1) * pair * PB)
        value = acc[rows, :] + products(3, rows)
        wait_bytes(recv_sem.at[RS_PC + i], pc_in.at[i])
        value = value + pc_in[i].astype(F32).reshape(pair * PB, CW)
        for h in range(pair):
            t = i * pair + h
            part_p = value[h * PB : (h + 1) * PB]
            if t == Z - 1:
                total = part_p
            else:
                pz_out[t] = part_p.astype(BF16)
                send(RS_PZ, RS_PZ, pz_out.at[t], pz_in.at[t], shifted(dz=Z - z_steps[t]))
    unfinished.append((RS_PZ, pz_in))
    wait_bytes(recv_sem.at[RS_PZ], pz_in)
    for t in range(Z - 1):
        total = total + pz_in[t].astype(F32)
    pressure = total.astype(BF16)
    prs_ref[...] = pressure
    weighted = (area_b[...] * pressure.astype(F32)).astype(BF16)

    for k in range(KB):
        cbuf[k] = (
            jnp.dot(shp_t[k], weighted, preferred_element_type=F32)
            .astype(BF16)
            .reshape(2, X, RW, CW)
        )
    other = 1 - core
    for n, dy in enumerate(y_steps):
        y_ = lax.rem(y + dy, Y)
        first = lax.rem(y_, YL) * (Z * YH) + lax.div(y_, YL)
        for zz in range(Z):
            lc_out[n, zz] = cbuf[inv[first + zz * YH], other]
        send(RS_LC, RS_LC + n, lc_out.at[n], lc_in.at[n], shifted(dc=1))
    unfinished.append((RS_LC, lc_out))
    lx_slot = 0
    for n, dy in enumerate(y_steps):
        y_ = lax.rem(y + dy, Y)
        first = lax.rem(y_, YL) * (Z * YH) + lax.div(y_, YL)
        wait_bytes(recv_sem.at[RS_LC + n], lc_in.at[n])
        for zz in range(Z):
            both = cbuf[inv[first + zz * YH], core].astype(F32) + lc_in[n, zz].astype(F32)
            for xx in range(X):
                lx_out[n, xx, zz] = both[xx].astype(BF16)
                if dy == 0:
                    lx_own[xx, zz] = both[xx]
        for dx in sorted(range(X), key=lambda q: -near(q, X)):
            if dx or dy:
                place = shifted(dx=dx, dy=dy)
                send(RS_LXY, RS_LXY, lx_out.at[n, place[0]], lx_in.at[lx_slot], place)
                lx_slot += 1
    unfinished.append((RS_LXY, lx_in))
    wait_bytes(recv_sem.at[RS_LXY], lx_in)
    lsum = lx_own[x]
    for q in range(n_xy - 1):
        lsum = lsum + lx_in[q].astype(F32)
    lx_own[x] = lsum
    lz_out[...] = lsum.astype(BF16)
    for t, dz in enumerate(z_steps[:-1]):
        place = shifted(dz=dz)
        send(RS_LZ, RS_LZ, lz_out.at[place[2]], lz_in.at[t], place)
    unfinished.append((RS_LZ, lz_in))
    fin = lx_own[x, z]
    wait_bytes(recv_sem.at[RS_LZ], lz_in)
    for t in range(Z - 1):
        fin = fin + lz_in[t].astype(F32)
    out_ref[...] = fin
    finish()


def copy_kernel(a_ref, b_ref, c_ref, d_ref):
    c_ref[...] = a_ref[...]
    d_ref[...] = b_ref[...]


def solution(mesh):
    Z = mesh.shape["blk"] // YL
    YH = mesh.shape["tgt"] // 2
    X = mesh.shape["sec"]
    Y = YH * YL
    n_xy, n_zc, n_blk = X * Y, 2 * Z, YL * Z
    mb = Z * RW

    def on_device(modal_loads, receptance, shapes, coupling, panel_coords, panel_areas):
        KB = shapes.shape[1]
        scratch = [
            pltpu.VMEM((n_xy, 8, PB), F32),
            pltpu.VMEM((n_zc, 8, PB), F32),
            pltpu.VMEM((3, n_zc * PB, PB), F32),
            pltpu.VMEM((PB, PB), F32),
            pltpu.VMEM((n_xy, n_zc * PB, 2 * PB), BF16),
            pltpu.VMEM((n_zc * PB, CW), F32),
            pltpu.VMEM((n_blk, RW, CW), F32),
            pltpu.VMEM((n_blk, RW, CW), BF16),
            pltpu.VMEM((n_blk - 1, RW, CW), BF16),
            pltpu.VMEM((YH, 2, X * YL, Z, RW, CW), BF16),
            pltpu.VMEM((n_xy, PB, CW), BF16),
            pltpu.VMEM((n_xy, 2 * PB, CW), BF16),
            pltpu.VMEM((Z // 2, 2, PB, CW), BF16),
            pltpu.VMEM((Z // 2, 2, PB, CW), BF16),
            pltpu.VMEM((Z - 1, PB, CW), BF16),
            pltpu.VMEM((Z - 1, PB, CW), BF16),
            pltpu.VMEM((PB * KB, mb), F32),
            pltpu.VMEM((KB, PB, mb), BF16),
            pltpu.VMEM((KB, mb, PB), BF16),
            pltpu.SMEM((n_blk * YH,), jnp.int32),
            pltpu.VMEM((KB + 1, 2, X, RW, CW), BF16),
            pltpu.VMEM((Y, Z, X, RW, CW), BF16),
            pltpu.VMEM((Y, Z, X, RW, CW), BF16),
            pltpu.VMEM((Y, X, Z, RW, CW), BF16),
            pltpu.VMEM((n_xy - 1, Z, RW, CW), BF16),
            pltpu.VMEM((X, Z, RW, CW), F32),
            pltpu.VMEM((Z, RW, CW), BF16),
            pltpu.VMEM((Z - 1, RW, CW), BF16),
            pltpu.SemaphoreType.DMA((N_SEM,)),
            pltpu.SemaphoreType.DMA((N_SEM,)),
        ]
        vmem = pl.BlockSpec(memory_space=pltpu.VMEM)
        outs = (
            jax.ShapeDtypeStruct((RW, CW), F32),
            jax.ShapeDtypeStruct((PB, CW), BF16),
        )
        results = pl.pallas_call(
            functools.partial(kernel, (X, YH, Z, KB)),
            out_shape=outs,
            in_specs=[vmem, vmem, vmem, pl.BlockSpec(memory_space=pltpu.SMEM), vmem, vmem],
            out_specs=(vmem, vmem),
            scratch_shapes=scratch,
            compiler_params=pltpu.CompilerParams(
                collective_id=0,
                has_side_effects=True,
                vmem_limit_bytes=58 * 1024 * 1024,
            ),
        )(
            modal_loads,
            receptance,
            shapes,
            coupling,
            panel_coords,
            panel_areas.reshape(1, PB),
        )
        return pl.pallas_call(
            copy_kernel,
            out_shape=outs,
            in_specs=[vmem, vmem],
            out_specs=(vmem, vmem),
        )(*results)

    owned = ("blk", "tgt", "sec")
    in_specs = (
        P("blk", None),
        P(None, ("tgt", "sec"), "blk"),
        P(owned, None, None),
        P(owned, None),
        P(None, owned),
        P(owned),
    )
    return jax.shard_map(
        on_device,
        mesh=mesh,
        in_specs=in_specs,
        out_specs=(P(owned, None), P(owned, None)),
        check_vma=False,
    )
```

time: 93.7 us -> 79.1 us (0.84)
  Pallas kernels: 88.5 us -> 78.3 us
  local copies, waits for them, and re-layouts: 4.35 us -> 0 us
    pallas_call x1 -> x2, Pallas kernels: 88.5 us -> 78.3 us  [the longest x1 76.9 us: on_device(): pl.pallas_call(functools.partial(kernel, (X, YH, Z, KB)), out_shape=outs,...]
    unnamed x3 -> x0, local copies, waits for them, and re-layouts: 4.35 us -> none
where the time goes in v2:
time: 79.1 us; the launch traced here: 79 us
  Pallas kernels  78.3 us (99%)
    pallas_call x1, Pallas kernels, on_device(): pl.pallas_call(functools.partial(kernel, (X, YH, Z, KB)), out_shape=outs,...  76.9 us

profile of v2, /device:TPU:1, one launch (start us, length us, event | category | flops | bytes accessed | tf_op | source)
XLA Modules:
  0.0 79.0 jit_solution(14591511714612160045)
XLA Ops:
  0.6 76.9 %shard_map.77 = (f32[16,128]{1,0:T(8,128)}, bf16[128,128]{1,0:T(8,128)(2,1)}) custom-call(bf16[256,128]{1,0:T(8,128)(2,1)} %loads_ref.1, bf16[2,256,256]{2,1,0:T(8,128)(2,1)} %rec_ref.1, bf16[128,8,128]{2,1,0:T(8,128)(2,1)} %shp_ref.1, s32[1,8]{1,0:T(1,128)} %cpl_ref.1, f32[3,128]{1,0:T(4,128)} %crd_ref.1, f32[1,128]{1,0:T(1,128)} %bitcast.1), custom_call_target="tpu_custom_call" | custom-call | tf_op jit(solution)/shard_map/pallas_call | solution.py:467
  77.6 1.4 %shard_map.78 = (f32[16,128]{1,0:T(8,128)}, bf16[128,128]{1,0:T(8,128)(2,1)}) custom-call(f32[16,128]{1,0:T(8,128)} %get-tuple-element.4.a_ref, bf16[128,128]{1,0:T(8,128)(2,1)} %get-tuple-element.5.b_ref), custom_call_target="tpu_custom_call" | custom-call | tf_op jit(solution)/shard_map/pallas_call | solution.py:486

commit v3 on v2

--- a/solution.py
+++ b/solution.py
@@ -19,13 +19,13 @@
 RW = 16
 ROWS = 128
 
-CUTS = (0, 3, 5, 7, 9, 11, 12, 14)
+CUTS = (2, 4, 7, 9, 10, 11, 12, 13, 16)
 
 SIN = (4.442879567546083, -7.307816684491776, 3.5977741780871795, -0.7911993921612632)
 COS = (1.4142040148090755, -6.977637323456285, 5.715187874756681, -1.7282138922234693)
 
-GEO_S, GEO_T, RS_AMP, AG_Z, AG_C, RS_PZ, RS_LXY, RS_LZ, AG_XY, VEL, RS_PC, RS_LC, N_SEM = (
-    0, 1, 2, 3, 4, 5, 6, 7, 8, 12, 16, 20, 24,
+GEO_S, GEO_T, RS_AMP, AG_Z, AG_C, RS_PZ, RS_LXY, RS_LZ, AG_XY, VEL, RS_PC, RS_LC, INP, N_SEM = (
+    0, 1, 2, 3, 4, 5, 6, 7, 8, 12, 16, 20, 24, 30,
 )
 
 
@@ -54,14 +54,20 @@
 
 def kernel(
     dims,
+    loads_hbm,
+    rec_hbm,
+    shp_hbm,
+    cpl_hbm,
+    crd_hbm,
+    area_hbm,
+    out_ref,
+    prs_ref,
     loads_ref,
     rec_ref,
     shp_ref,
     cpl_ref,
     crd_ref,
     area_ref,
-    out_ref,
-    prs_ref,
     geo_s,
     geo_t,
     tgt_b,
@@ -123,7 +129,8 @@
     blk_steps = sorted(
         ((dl, dz) for dl in range(YL) for dz in range(Z) if dl or dz), key=lambda s: -s[0] - near(s[1], Z)
     )
-    groups = [range(n_xy * g // 4, n_xy * (g + 1) // 4) for g in range(4)]
+    edges = (0, min(5, n_xy - 2), min(11, n_xy - 1), n_xy)
+    groups = [range(lo, hi) for lo, hi in zip(edges, edges[1:])]
 
     def yl_place(dl, dz):
         y_ = yh * YL + lax.rem(yl + dl, YL)
@@ -155,11 +162,29 @@
     for place in places:
         pl.semaphore_signal(barrier, inc=1, device_id=device(*place), device_id_type=MESH)
 
+    inputs = [
+        pltpu.make_async_copy(src, dst, recv_sem.at[INP + i])
+        for i, (src, dst) in enumerate(
+            (
+                (crd_hbm, crd_ref),
+                (area_hbm, area_ref),
+                (loads_hbm, loads_ref),
+                (rec_hbm, rec_ref),
+                (shp_hbm, shp_ref),
+                (cpl_hbm, cpl_ref),
+            )
+        )
+    ]
+    for copy in inputs:
+        copy.start()
+    inputs[0].wait()
+    inputs[1].wait()
     half_scale = 0.5 * WAVE / math.pi
     geo_s[0, 0:3, :] = crd_ref[...] * half_scale
     geo_s[0, 3:4, :] = area_ref[...] * (half_scale * half_scale / total_panels)
-    geo_s[0, 4:8, :] = jnp.zeros((4, PB), F32)
     geo_t[n_zc - 1, :, :] = geo_s[0, :, :]
+    inputs[2].wait()
+    inputs[3].wait()
     loads = loads_ref[...]
     loads_rot = rotated(loads.astype(F32)).astype(BF16)
     psum = jnp.dot(rec_ref[0], loads, preferred_element_type=F32) + jnp.dot(
@@ -184,33 +209,31 @@
     unfinished.append((GEO_T, geo_t.at[pl.ds(1, n_zc - 1)]))
     unfinished.append((RS_AMP, amp_in))
 
-    area_b[...] = turn_rows(area_ref[...])
-    shp_f[...] = shp_ref[...].astype(F32).reshape(PB * KB, mb)
-    for k in range(KB):
-        block = shp_f[pl.ds(k, PB, stride=KB), :]
-        shp_k[k] = block.astype(BF16)
-        shp_t[k] = jnp.transpose(block).astype(BF16)
-    cbuf[KB] = jnp.zeros((2, X, RW, CW), BF16)
-
-    def fill_inv(j, carry):
-        found = jnp.int32(KB)
+    def prepare():
+        inputs[4].wait()
+        area_b[...] = turn_rows(area_ref[...])
+        shp_f[...] = shp_ref[...].astype(F32).reshape(PB * KB, mb)
         for k in range(KB):
-            found = jnp.where(cpl_ref[0, k] == j, jnp.int32(k), found)
-        inv[j] = found
-        return carry
-
-    lax.fori_loop(0, n_blk * YH, fill_inv, 0)
-
-    wait_bytes(recv_sem.at[GEO_T], geo_t.at[pl.ds(1, n_zc - 1)])
+            block = shp_f[pl.ds(k, PB, stride=KB), :]
+            shp_k[k] = block.astype(BF16)
+            shp_t[k] = jnp.transpose(block).astype(BF16)
+        cbuf[KB] = jnp.zeros((2, X, RW, CW), BF16)
+        inputs[5].wait()
+
+        def fill_inv(j, carry):
+            found = jnp.int32(KB)
+            for k in range(KB):
+                found = jnp.where(cpl_ref[0, k] == j, jnp.int32(k), found)
+            inv[j] = found
+            return carry
+
+        lax.fori_loop(0, n_blk * YH, fill_inv, 0)
 
     def turn_step(slot, carry):
         rows = pl.ds(pl.multiple_of(slot * PB, PB), PB)
         for axis in range(3):
             tgt_b[axis, rows, :] = turn_rows(geo_t[slot, axis : axis + 1, :])
         return carry
-
-    lax.fori_loop(0, n_zc, turn_step, 0)
-    wait_bytes(recv_sem.at[GEO_S], geo_s.at[pl.ds(1, n_xy - 1)])
 
     steps = n_zc * PB // ROWS
 
@@ -245,7 +268,7 @@
 
     cuts = [round(n_xy * part_of / 16) for part_of in CUTS]
 
-    kernel_chunks(cuts[0], cuts[1])
+    prepare()
 
     wait_bytes(recv_sem.at[RS_AMP], amp_in)
     asum = part[blk]
@@ -259,20 +282,29 @@
     seven = amp.at[0, 0, 0, pl.ds(0, Z - 1)]
     unfinished.append((AG_Z, seven))
 
-    kernel_chunks(cuts[1], cuts[2])
+    wait_bytes(recv_sem.at[GEO_T], geo_t.at[pl.ds(1, n_zc - 1)])
+    lax.fori_loop(0, n_zc, turn_step, 0)
+    wait_bytes(recv_sem.at[GEO_S], geo_s.at[pl.ds(1, n_xy - 1)])
+    kernel_chunks(0, cuts[0])
     wait_bytes(recv_sem.at[AG_Z], seven)
     mine = amp.at[yh, core, xl]
-    for g, group in enumerate(groups):
-        for n in group:
+
+    def send_block(g):
+        for n in groups[g]:
             dx, dy = xy_steps[n]
             if n:
                 send(AG_XY, AG_XY + g, mine, mine, shifted(dx=dx, dy=dy))
+
+    send_block(2)
+    send_block(1)
+    send(AG_C, AG_C, mine, mine, shifted(dc=1))
+    kernel_chunks(cuts[0], cuts[1])
+    send_block(0)
     unfinished.append((AG_XY, vels.at[pl.ds(1, n_xy - 1), pl.ds(0, mb)]))
-    send(AG_C, AG_C, mine, mine, shifted(dc=1))
-
-    for g, group in enumerate(groups):
-        kernel_chunks(cuts[2 + g], cuts[3 + g])
-        rest = [n for n in group if n]
+
+    for i, g in enumerate((2, 1, 0)):
+        kernel_chunks(cuts[1 + i], cuts[2 + i])
+        rest = [n for n in groups[g] if n]
         if not rest:
             continue
         wait_bytes(recv_sem.at[AG_XY + g], vels.at[pl.ds(1, len(rest)), pl.ds(0, mb)])
@@ -283,7 +315,7 @@
             send(AG_C, AG_C, theirs, theirs, shifted(dc=1))
     half_amp = amp.at[:, 0]
     unfinished.append((AG_C, half_amp))
-    kernel_chunks(cuts[6], cuts[7])
+    kernel_chunks(cuts[4], cuts[5])
     wait_bytes(recv_sem.at[AG_C], half_amp)
 
     vel = jnp.zeros((PB, CW), F32)
@@ -300,8 +332,8 @@
             dx, dy = xy_steps[n]
             if n:
                 send(VEL, VEL + g, vels.at[0], vels.at[n], shifted(dx=dx, dy=dy))
+        kernel_chunks(cuts[5 + g], cuts[6 + g])
     unfinished.append((VEL, vels.at[pl.ds(1, n_xy - 1)]))
-    kernel_chunks(cuts[7], n_xy)
 
     def weights(g):
         group = groups[g]
@@ -320,8 +352,9 @@
             total = term if total is None else total + term
         return total
 
-    mm_rows = min(512, n_zc * PB)
-    for g in range(3):
+    mm_rows = min(1024, n_zc * PB)
+    last = len(groups) - 1
+    for g in range(last):
         weights(g)
 
         def mm_step(i, carry):
@@ -332,29 +365,49 @@
 
         lax.fori_loop(0, n_zc * PB // mm_rows, mm_step, 0)
 
-    weights(3)
+    weights(last)
     pair = 2
     n_pair = Z // pair
-    for i in range(n_pair):
-        rows = slice(i * pair * PB, (i + 1) * pair * PB)
-        value = acc[rows, :] + products(3, rows)
+
+    def other_core(i):
+        rows = pl.ds(pl.multiple_of(i * (pair * PB), pair * PB), pair * PB)
+        value = acc[rows, :] + products(last, rows)
         p_out[i] = value.astype(BF16).reshape(pair, PB, CW)
         send(RS_PC, RS_PC + i, p_out.at[i], pc_in.at[i], shifted(dc=1))
-    unfinished.append((RS_PC, p_out))
-    total = None
-    for i in range(n_pair):
-        rows = slice((n_pair + i) * pair * PB, (n_pair + i + 1) * pair * PB)
-        value = acc[rows, :] + products(3, rows)
+
+    def this_core(i, final=False):
+        rows = pl.ds(pl.multiple_of((n_pair + i) * (pair * PB), pair * PB), pair * PB)
+        value = acc[rows, :] + products(last, rows)
         wait_bytes(recv_sem.at[RS_PC + i], pc_in.at[i])
         value = value + pc_in[i].astype(F32).reshape(pair * PB, CW)
         for h in range(pair):
             t = i * pair + h
             part_p = value[h * PB : (h + 1) * PB]
-            if t == Z - 1:
-                total = part_p
-            else:
-                pz_out[t] = part_p.astype(BF16)
-                send(RS_PZ, RS_PZ, pz_out.at[t], pz_in.at[t], shifted(dz=Z - z_steps[t]))
+            if final and h == pair - 1:
+                return part_p
+            back = Z // 2 + i + 1 if h else Z // 2 - i
+            pz_out[t] = part_p.astype(BF16)
+            send(RS_PZ, RS_PZ, pz_out.at[t], pz_in.at[t], shifted(dz=back))
+
+    def first_steps(i, carry):
+        other_core(i)
+        return carry
+
+    def middle_steps(i, carry):
+        other_core(i + ahead)
+        this_core(i)
+        return carry
+
+    def later_steps(i, carry):
+        this_core(i)
+        return carry
+
+    ahead = min(2, n_pair)
+    lax.fori_loop(0, ahead, first_steps, 0)
+    lax.fori_loop(0, n_pair - ahead, middle_steps, 0)
+    lax.fori_loop(n_pair - ahead, n_pair - 1, later_steps, 0)
+    total = this_core(n_pair - 1, final=True)
+    unfinished.append((RS_PC, p_out))
     unfinished.append((RS_PZ, pz_in))
     wait_bytes(recv_sem.at[RS_PZ], pz_in)
     for t in range(Z - 1):
@@ -428,8 +481,14 @@
     def on_device(modal_loads, receptance, shapes, coupling, panel_coords, panel_areas):
         KB = shapes.shape[1]
         scratch = [
-            pltpu.VMEM((n_xy, 8, PB), F32),
-            pltpu.VMEM((n_zc, 8, PB), F32),
+            pltpu.VMEM(modal_loads.shape, BF16),
+            pltpu.VMEM(receptance.shape, BF16),
+            pltpu.VMEM(shapes.shape, BF16),
+            pltpu.SMEM(coupling.shape, jnp.int32),
+            pltpu.VMEM(panel_coords.shape, F32),
+            pltpu.VMEM((1, PB), F32),
+            pltpu.VMEM((n_xy, 4, PB), F32),
+            pltpu.VMEM((n_zc, 4, PB), F32),
             pltpu.VMEM((3, n_zc * PB, PB), F32),
             pltpu.VMEM((PB, PB), F32),
             pltpu.VMEM((n_xy, n_zc * PB, 2 * PB), BF16),
@@ -467,7 +526,7 @@
         results = pl.pallas_call(
             functools.partial(kernel, (X, YH, Z, KB)),
             out_shape=outs,
-            in_specs=[vmem, vmem, vmem, pl.BlockSpec(memory_space=pltpu.SMEM), vmem, vmem],
+            in_specs=[pl.BlockSpec(memory_space=pl.ANY)] * 6,
             out_specs=(vmem, vmem),
             scratch_shapes=scratch,
             compiler_params=pltpu.CompilerParams(

time: 79.1 us -> 71.3 us (0.901)
  Pallas kernels: 78.3 us -> 70.5 us
    pallas_call x1, Pallas kernels: 76.9 us -> 69.1 us  [on_device(): pl.pallas_call(functools.partial(kernel, (X, YH, Z, KB)), out_shape=outs,...]
where the time goes in v3:
time: 71.3 us; the launch traced here: 71.1 us
  Pallas kernels  70.5 us (99%)
    pallas_call x1, Pallas kernels, on_device(): pl.pallas_call(functools.partial(kernel, (X, YH, Z, KB)), out_shape=outs,...  69.1 us

profile of v3, /device:TPU:1, one launch (start us, length us, event | category | flops | bytes accessed | tf_op | source)
XLA Modules:
  0.0 71.1 jit_solution(18214253890082937210)
XLA Ops:
  0.6 69.1 %shard_map.77 = (f32[16,128]{1,0:T(8,128)}, bf16[128,128]{1,0:T(8,128)(2,1)}) custom-call(bf16[256,128]{1,0:T(8,128)(2,1)} %loads_hbm.1, bf16[2,256,256]{2,1,0:T(8,128)(2,1)} %rec_hbm.1, bf16[128,8,128]{2,1,0:T(8,128)(2,1)} %shp_hbm.1, s32[1,8]{1,0:T(1,128)} %cpl_hbm.1, f32[3,128]{1,0:T(4,128)} %crd_hbm.1, f32[1,128]{1,0:T(1,128)} %bitcast.1), custom_call_target="tpu_custom_call" | custom-call | tf_op jit(solution)/shard_map/pallas_call | solution.py:526
  69.7 1.4 %shard_map.78 = (f32[16,128]{1,0:T(8,128)}, bf16[128,128]{1,0:T(8,128)(2,1)}) custom-call(f32[16,128]{1,0:T(8,128)} %get-tuple-element.4.a_ref, bf16[128,128]{1,0:T(8,128)(2,1)} %get-tuple-element.5.b_ref), custom_call_target="tpu_custom_call" | custom-call | tf_op jit(solution)/shard_map/pallas_call | solution.py:545

commit v4 on v3

--- a/solution.py
+++ b/solution.py
@@ -17,9 +17,9 @@
 PB = 128
 CW = 128
 RW = 16
-ROWS = 128
-
-CUTS = (2, 4, 7, 9, 10, 11, 12, 13, 16)
+ROWS = 256
+
+CUTS = (2, 4, 7, 9, 10, 11)
 
 SIN = (4.442879567546083, -7.307816684491776, 3.5977741780871795, -0.7911993921612632)
 COS = (1.4142040148090755, -6.977637323456285, 5.715187874756681, -1.7282138922234693)
@@ -130,7 +130,9 @@
         ((dl, dz) for dl in range(YL) for dz in range(Z) if dl or dz), key=lambda s: -s[0] - near(s[1], Z)
     )
     edges = (0, min(5, n_xy - 2), min(11, n_xy - 1), n_xy)
+    used = (0, min(5, n_xy - 2), min(13, n_xy - 1), n_xy)
     groups = [range(lo, hi) for lo, hi in zip(edges, edges[1:])]
+    batches = [range(lo, hi) for lo, hi in zip(used, used[1:])]
 
     def yl_place(dl, dz):
         y_ = yh * YL + lax.rem(yl + dl, YL)
@@ -275,9 +277,9 @@
     for q in range(n_blk - 1):
         asum = asum + amp_in[q].astype(F32)
     xl = x * YL + yl
-    amp[yh, core, xl, z] = asum.astype(BF16)
+    amp[core, yh, xl, z] = asum.astype(BF16)
     for dz in z_steps[:-1]:
-        mine = amp.at[yh, core, xl, z]
+        mine = amp.at[core, yh, xl, z]
         send(AG_Z, AG_Z, mine, mine, shifted(dz=dz))
     seven = amp.at[0, 0, 0, pl.ds(0, Z - 1)]
     unfinished.append((AG_Z, seven))
@@ -287,7 +289,7 @@
     wait_bytes(recv_sem.at[GEO_S], geo_s.at[pl.ds(1, n_xy - 1)])
     kernel_chunks(0, cuts[0])
     wait_bytes(recv_sem.at[AG_Z], seven)
-    mine = amp.at[yh, core, xl]
+    mine = amp.at[core, yh, xl]
 
     def send_block(g):
         for n in groups[g]:
@@ -297,23 +299,16 @@
 
     send_block(2)
     send_block(1)
-    send(AG_C, AG_C, mine, mine, shifted(dc=1))
     kernel_chunks(cuts[0], cuts[1])
     send_block(0)
     unfinished.append((AG_XY, vels.at[pl.ds(1, n_xy - 1), pl.ds(0, mb)]))
-
-    for i, g in enumerate((2, 1, 0)):
-        kernel_chunks(cuts[1 + i], cuts[2 + i])
+    kernel_chunks(cuts[1], cuts[4])
+    for g in (2, 1, 0):
         rest = [n for n in groups[g] if n]
-        if not rest:
-            continue
-        wait_bytes(recv_sem.at[AG_XY + g], vels.at[pl.ds(1, len(rest)), pl.ds(0, mb)])
-        for n in rest:
-            dx, dy = xy_steps[n]
-            sx, sy = lax.rem(x + X - dx, X), lax.rem(y + Y - dy, Y)
-            theirs = amp.at[lax.div(sy, YL), core, sx * YL + lax.rem(sy, YL)]
-            send(AG_C, AG_C, theirs, theirs, shifted(dc=1))
-    half_amp = amp.at[:, 0]
+        if rest:
+            wait_bytes(recv_sem.at[AG_XY + g], vels.at[pl.ds(1, len(rest)), pl.ds(0, mb)])
+    half_amp = amp.at[core]
+    send(AG_C, AG_C, half_amp, half_amp, shifted(dc=1))
     unfinished.append((AG_C, half_amp))
     kernel_chunks(cuts[4], cuts[5])
     wait_bytes(recv_sem.at[AG_C], half_amp)
@@ -324,19 +319,20 @@
         jl = lax.rem(j, X * YL)
         jc = lax.rem(lax.div(j, X * YL), 2)
         jh = lax.div(j, X * YL * 2)
-        block = amp[jh, jc, jl].reshape(mb, CW)
+        block = amp[jc, jh, jl].reshape(mb, CW)
         vel = vel + jnp.dot(shp_k[k], block, preferred_element_type=F32)
     vels[0] = (vel * area_b[...] * (half_scale / math.sqrt(total_panels))).astype(BF16)
     for g, group in enumerate(groups):
         for n in group:
             dx, dy = xy_steps[n]
             if n:
-                send(VEL, VEL + g, vels.at[0], vels.at[n], shifted(dx=dx, dy=dy))
-        kernel_chunks(cuts[5 + g], cuts[6 + g])
+                batch = [n in b for b in batches].index(True)
+                send(VEL, VEL + batch, vels.at[0], vels.at[n], shifted(dx=dx, dy=dy))
+    kernel_chunks(cuts[5], n_xy)
     unfinished.append((VEL, vels.at[pl.ds(1, n_xy - 1)]))
 
     def weights(g):
-        group = groups[g]
+        group = batches[g]
         rest = [n for n in group if n]
         if rest:
             wait_bytes(recv_sem.at[VEL + g], vels.at[pl.ds(rest[0], len(rest))])
@@ -347,13 +343,13 @@
 
     def products(g, rows):
         total = None
-        for n in groups[g]:
+        for n in batches[g]:
             term = jnp.dot(kmat[n, rows, :], w_ref[n], preferred_element_type=F32)
             total = term if total is None else total + term
         return total
 
     mm_rows = min(1024, n_zc * PB)
-    last = len(groups) - 1
+    last = len(batches) - 1
     for g in range(last):
         weights(g)
 
@@ -496,7 +492,7 @@
             pltpu.VMEM((n_blk, RW, CW), F32),
             pltpu.VMEM((n_blk, RW, CW), BF16),
             pltpu.VMEM((n_blk - 1, RW, CW), BF16),
-            pltpu.VMEM((YH, 2, X * YL, Z, RW, CW), BF16),
+            pltpu.VMEM((2, YH, X * YL, Z, RW, CW), BF16),
             pltpu.VMEM((n_xy, PB, CW), BF16),
             pltpu.VMEM((n_xy, 2 * PB, CW), BF16),
             pltpu.VMEM((Z // 2, 2, PB, CW), BF16),

time: 71.3 us -> 70.3 us (0.986)
  Pallas kernels: 70.5 us -> 69.5 us
    pallas_call x1, Pallas kernels: 69.1 us -> 68.1 us  [on_device(): pl.pallas_call(functools.partial(kernel, (X, YH, Z, KB)), out_shape=outs,...]
where the time goes in v4:
time: 70.3 us; the launch traced here: 70.2 us
  Pallas kernels  69.5 us (99%)
    pallas_call x1, Pallas kernels, on_device(): pl.pallas_call(functools.partial(kernel, (X, YH, Z, KB)), out_shape=outs,...  68.1 us

profile of v4, /device:TPU:1, one launch (start us, length us, event | category | flops | bytes accessed | tf_op | source)
XLA Modules:
  0.0 70.2 jit_solution(11361222968326421699)
XLA Ops:
  0.6 68.1 %shard_map.77 = (f32[16,128]{1,0:T(8,128)}, bf16[128,128]{1,0:T(8,128)(2,1)}) custom-call(bf16[256,128]{1,0:T(8,128)(2,1)} %loads_hbm.1, bf16[2,256,256]{2,1,0:T(8,128)(2,1)} %rec_hbm.1, bf16[128,8,128]{2,1,0:T(8,128)(2,1)} %shp_hbm.1, s32[1,8]{1,0:T(1,128)} %cpl_hbm.1, f32[3,128]{1,0:T(4,128)} %crd_hbm.1, f32[1,128]{1,0:T(1,128)} %bitcast.1), custom_call_target="tpu_custom_call" | custom-call | tf_op jit(solution)/shard_map/pallas_call | solution.py:522
  68.8 1.4 %shard_map.78 = (f32[16,128]{1,0:T(8,128)}, bf16[128,128]{1,0:T(8,128)(2,1)}) custom-call(f32[16,128]{1,0:T(8,128)} %get-tuple-element.4.a_ref, bf16[128,128]{1,0:T(8,128)(2,1)} %get-tuple-element.5.b_ref), custom_call_target="tpu_custom_call" | custom-call | tf_op jit(solution)/shard_map/pallas_call | solution.py:541

commit v5 on v4

--- a/solution.py
+++ b/solution.py
@@ -130,7 +130,7 @@
         ((dl, dz) for dl in range(YL) for dz in range(Z) if dl or dz), key=lambda s: -s[0] - near(s[1], Z)
     )
     edges = (0, min(5, n_xy - 2), min(11, n_xy - 1), n_xy)
-    used = (0, min(5, n_xy - 2), min(13, n_xy - 1), n_xy)
+    used = (0, min(5, n_xy - 2), min(11, n_xy - 1), n_xy)
     groups = [range(lo, hi) for lo, hi in zip(edges, edges[1:])]
     batches = [range(lo, hi) for lo, hi in zip(used, used[1:])]
 

time: 70.3 us -> 69.5 us (0.989)
  Pallas kernels: 69.5 us -> 68.6 us
    pallas_call x1, Pallas kernels: 68.1 us -> 67.2 us  [on_device(): pl.pallas_call(functools.partial(kernel, (X, YH, Z, KB)), out_shape=outs,...]
where the time goes in v5:
time: 69.5 us; the launch traced here: 69.3 us
  Pallas kernels  68.6 us (99%)
    pallas_call x1, Pallas kernels, on_device(): pl.pallas_call(functools.partial(kernel, (X, YH, Z, KB)), out_shape=outs,...  67.2 us
    pallas_call x1, Pallas kernels, on_device(): pl.pallas_call(copy_kernel, out_shape=outs, in_specs=[vmem, vmem], out_sp...  1.4 us

profile of v5, /device:TPU:1, one launch (start us, length us, event | category | flops | bytes accessed | tf_op | source)
XLA Modules:
  0.0 69.3 jit_solution(2854287364483164554)
XLA Ops:
  0.6 67.2 %shard_map.77 = (f32[16,128]{1,0:T(8,128)}, bf16[128,128]{1,0:T(8,128)(2,1)}) custom-call(bf16[256,128]{1,0:T(8,128)(2,1)} %loads_hbm.1, bf16[2,256,256]{2,1,0:T(8,128)(2,1)} %rec_hbm.1, bf16[128,8,128]{2,1,0:T(8,128)(2,1)} %shp_hbm.1, s32[1,8]{1,0:T(1,128)} %cpl_hbm.1, f32[3,128]{1,0:T(4,128)} %crd_hbm.1, f32[1,128]{1,0:T(1,128)} %bitcast.1), custom_call_target="tpu_custom_call" | custom-call | tf_op jit(solution)/shard_map/pallas_call | solution.py:522
  67.9 1.4 %shard_map.78 = (f32[16,128]{1,0:T(8,128)}, bf16[128,128]{1,0:T(8,128)(2,1)}) custom-call(f32[16,128]{1,0:T(8,128)} %get-tuple-element.4.a_ref, bf16[128,128]{1,0:T(8,128)(2,1)} %get-tuple-element.5.b_ref), custom_call_target="tpu_custom_call" | custom-call | tf_op jit(solution)/shard_map/pallas_call | solution.py:541

commit v6 on v5

--- a/solution.py
+++ b/solution.py
@@ -130,7 +130,7 @@
         ((dl, dz) for dl in range(YL) for dz in range(Z) if dl or dz), key=lambda s: -s[0] - near(s[1], Z)
     )
     edges = (0, min(5, n_xy - 2), min(11, n_xy - 1), n_xy)
-    used = (0, min(5, n_xy - 2), min(11, n_xy - 1), n_xy)
+    used = (0, min(5, n_xy - 2), min(10, n_xy - 1), n_xy)
     groups = [range(lo, hi) for lo, hi in zip(edges, edges[1:])]
     batches = [range(lo, hi) for lo, hi in zip(used, used[1:])]
 

time: 69.5 us -> 69.3 us (level)
  no operation moved by 1% of the time
where the time goes in v6:
time: 69.3 us; the launch traced here: 69.1 us
  Pallas kernels  68.5 us (99%)
    pallas_call x1, Pallas kernels, on_device(): pl.pallas_call(functools.partial(kernel, (X, YH, Z, KB)), out_shape=outs,...  67.1 us
    pallas_call x1, Pallas kernels, on_device(): pl.pallas_call(copy_kernel, out_shape=outs, in_specs=[vmem, vmem], out_sp...  1.4 us

profile of v6, /device:TPU:1, one launch (start us, length us, event | category | flops | bytes accessed | tf_op | source)
XLA Modules:
  0.0 69.1 jit_solution(11512649075415310491)
XLA Ops:
  0.6 67.1 %shard_map.77 = (f32[16,128]{1,0:T(8,128)}, bf16[128,128]{1,0:T(8,128)(2,1)}) custom-call(bf16[256,128]{1,0:T(8,128)(2,1)} %loads_hbm.1, bf16[2,256,256]{2,1,0:T(8,128)(2,1)} %rec_hbm.1, bf16[128,8,128]{2,1,0:T(8,128)(2,1)} %shp_hbm.1, s32[1,8]{1,0:T(1,128)} %cpl_hbm.1, f32[3,128]{1,0:T(4,128)} %crd_hbm.1, f32[1,128]{1,0:T(1,128)} %bitcast.1), custom_call_target="tpu_custom_call" | custom-call | tf_op jit(solution)/shard_map/pallas_call | solution.py:522
  67.7 1.4 %shard_map.78 = (f32[16,128]{1,0:T(8,128)}, bf16[128,128]{1,0:T(8,128)(2,1)}) custom-call(f32[16,128]{1,0:T(8,128)} %get-tuple-element.4.a_ref, bf16[128,128]{1,0:T(8,128)(2,1)} %get-tuple-element.5.b_ref), custom_call_target="tpu_custom_call" | custom-call | tf_op jit(solution)/shard_map/pallas_call | solution.py:541
